TPU v7x, 256 devices: a whole 4x4x8 slice. The times are simulated.
256 devices in a mesh: row: 32 (over x, y, core), col: 8 (over z).
Axes of the slice: x: 4, y: 4, z: 8, core: 2. Of those that a mesh axis runs over, the one named last changes fastest.
Arguments:
- inputs: bfloat16 [16384, 1792], P(('row', 'col')), may hold values from -6 to 6
- attention_norm_gain: float32 [1792], replicated, may hold values from 0.5 to 1.5
- query_key_value_weight: bfloat16 [1792, 3, 1792], P('row', None, 'col'), may hold values from -0.125 to 0.125
- filter_taps: float32 [3, 2, 1792], P(None, None, 'col'), may hold values from -3 to 3
- output_projection: bfloat16 [1792, 1792], P('col', 'row'), may hold values from -0.125 to 0.125
- window_key_value: bfloat16 [256, 2, 16, 7168], P('row', None, 'col'), may hold values from -300 to 300
- cache_valid_length: int32 [256], P('row'), may hold values from 0 to 64
- lengths: int32 [32, 8], P('row'), may hold values from 1 to 128, 512 in all within a row
- token_adapter_index: int32 [16384, 1], P('row'), may hold values from 0 to 63; in each aligned block of 64 rows (0 to 63, 64 to 127, ...) at most 2 rows name the same one
- adapter_down_map: bfloat16 [64, 1792, 16], P('row'), may hold values from -0.125 to 0.125
- adapter_up_map: bfloat16 [64, 16, 1792], P('row'), may hold values from -1.5 to 1.5
- feed_forward_gain: float32 [1792], replicated, may hold values from 0.5 to 1.5
- gate_projection: bfloat16 [1792, 4096], P('row', 'col'), may hold values from -0.125 to 0.125
- up_projection: bfloat16 [1792, 4096], P('row', 'col'), may hold values from -0.125 to 0.125
- down_projection: bfloat16 [4096, 1792], P('col', 'row'), may hold values from -0.09375 to 0.09375
Outputs:
- layer_out: bfloat16 [16384, 1792], P(('row', 'col'))
Inputs may be any that keep to these rules, and one draw needn't show every extreme that they name: Each row of lengths sums to 512, and its largest entry is exactly 128. `cache_valid_length`: A request with 0 is a new prompt without cached positions. `token_adapter_index`: in each aligned block of 64 tokens no adapter serves more than 2 tokens, and some adapter serves exactly 2.
All inputs are finite; a program needn't handle non-finite values.
Results may differ from a plain program's by a relative error of at most 0.019.
Values may be sent and summed in bfloat16 or wider, within the bound.
A program may use at most 64 MiB of HBM per device.

v0:
```python
import jax
import jax.numpy as jnp
from jax import lax
from jax.sharding import PartitionSpec as P

HD = 112
epsilon = 1e-05


def rms_scaled(values, gain_row):
    mean_square = jnp.mean(values * values, axis=-1, keepdims=True)
    return values * lax.rsqrt(mean_square + epsilon) * gain_row


def layout(lengths_row, tok_count):
    finish = jnp.cumsum(lengths_row)
    begins = finish - lengths_row
    places = jnp.arange(tok_count, dtype=jnp.int32)
    segment = jnp.sum((places[:, None] >= finish[None, :]).astype(jnp.int32), axis=1)
    member = segment[:, None] == jnp.arange(lengths_row.shape[0], dtype=jnp.int32)[None, :]
    inside = places - jnp.sum(jnp.where(member, begins[None, :], 0), axis=1)
    return (segment, inside)


def shifted(values, offset, inside):
    moved_rows = jnp.pad(values[: values.shape[0] - offset], ((offset, 0), (0, 0)))
    return jnp.where((inside >= offset)[:, None], moved_rows, jnp.zeros_like(moved_rows))


def convolve(values, taps, inside):
    running = jnp.zeros_like(values)
    for offset in range(taps.shape[0]):
        running = running + taps[offset][None, :] * shifted(values, offset, inside)
    return running


def make_qkv(qkv_mixed, filter_taps, inside):
    queries = qkv_mixed[:, 0].astype(jnp.bfloat16)
    keys_used = convolve(qkv_mixed[:, 1], filter_taps[:, 0], inside).astype(jnp.bfloat16)
    raw_values = qkv_mixed[:, 2]
    gates = jax.nn.sigmoid(convolve(raw_values, filter_taps[:, 1], inside))
    values_used = (raw_values * gates).astype(jnp.bfloat16)
    return (queries, keys_used, values_used)


def split_cache(window_key_value, head_size):
    requests_here, head_count = (window_key_value.shape[0], window_key_value.shape[2])
    window = window_key_value.shape[3] // head_size
    split_kv = window_key_value.reshape(requests_here, 2, head_count, window, head_size)
    cached_key_rows = jnp.transpose(split_kv[:, 0], (0, 2, 1, 3)).reshape(
        requests_here * window, head_count, head_size
    )
    cached_value_rows = jnp.transpose(split_kv[:, 1], (0, 2, 1, 3)).reshape(
        requests_here * window, head_count, head_size
    )
    return (cached_key_rows, cached_value_rows, window)


def attend(
    queries,
    keys_used,
    values_used,
    window_key_value,
    segment,
    inside,
    cache_valid_length,
    head_size,
):
    tok_count = queries.shape[0]
    head_count = queries.shape[1] // head_size
    requests_here = window_key_value.shape[0]
    cached_key_rows, cached_value_rows, window = split_cache(window_key_value, head_size)
    query_per_head = queries.reshape(tok_count, head_count, head_size)
    key_h = keys_used.reshape(tok_count, head_count, head_size)
    value_per_head = values_used.reshape(tok_count, head_count, head_size)
    attention_score_scale = head_size ** (-0.5)
    places = jnp.arange(tok_count, dtype=jnp.int32)
    local_mask = (
        (segment[:, None] == segment[None, :])
        & (places[None, :] <= places[:, None])
        & (places[None, :] > places[:, None] - window)
    )
    slot_ids = jnp.arange(requests_here * window, dtype=jnp.int32)
    owner_req = slot_ids // window
    within = slot_ids % window
    slot_ages = jnp.repeat(cache_valid_length, window)
    cache_mask = (
        (segment[:, None] == owner_req[None, :])
        & (within[None, :] >= window - slot_ages[None, :])
        & (within[None, :] > inside[:, None])
    )
    local_scores = (
        jnp.einsum("thd,jhd->htj", query_per_head, key_h, preferred_element_type=jnp.float32)
        * attention_score_scale
    )
    cached_score_rows = (
        jnp.einsum(
            "sek,yek->esy", query_per_head, cached_key_rows, preferred_element_type=jnp.float32
        )
        * attention_score_scale
    )
    local_scores = jnp.where(local_mask[None], local_scores, -jnp.inf)
    cached_score_rows = jnp.where(cache_mask[None], cached_score_rows, -jnp.inf)
    row_max = jnp.maximum(
        jnp.max(local_scores, axis=-1, keepdims=True),
        jnp.max(cached_score_rows, axis=-1, keepdims=True),
    )
    local_exp = jnp.exp(local_scores - row_max)
    cache_exp = jnp.exp(cached_score_rows - row_max)
    denominator = jnp.sum(local_exp, axis=-1, keepdims=True) + jnp.sum(
        cache_exp, axis=-1, keepdims=True
    )
    window_attention_weight = (local_exp / denominator).astype(jnp.bfloat16)
    cached_attention_weight = (cache_exp / denominator).astype(jnp.bfloat16)
    joined_output = jnp.einsum(
        "zkc,czu->kzu", window_attention_weight, value_per_head, preferred_element_type=jnp.float32
    )
    joined_output = joined_output + jnp.einsum(
        "lar,rlx->alx",
        cached_attention_weight,
        cached_value_rows,
        preferred_element_type=jnp.float32,
    )
    return joined_output.reshape(tok_count, head_count * head_size).astype(jnp.bfloat16)


def on_device(
    inputs,
    attention_norm_gain,
    query_key_value_weight,
    filter_taps,
    output_projection,
    window_key_value,
    cache_valid_length,
    lengths,
    token_adapter_index,
    adapter_down_map,
    adapter_up_map,
    feed_forward_gain,
    gate_projection,
    up_projection,
    down_projection,
):
    own_count = inputs.shape[0]
    column = lax.axis_index("col")
    row_count = lax.axis_size("row")
    gathered = lax.all_gather(inputs, "col", axis=0, tiled=True)
    tok_count = gathered.shape[0]
    normalized_input = rms_scaled(gathered.astype(jnp.float32), attention_norm_gain).astype(
        jnp.bfloat16
    )
    qkv_mixed = jnp.einsum(
        "td,dka->tka",
        normalized_input,
        lax.all_gather(query_key_value_weight, "row", axis=0, tiled=True),
        preferred_element_type=jnp.float32,
    )
    segment, inside = layout(lengths[0], tok_count)
    queries, keys_used, values_used = make_qkv(qkv_mixed, filter_taps, inside)
    attended = attend(
        queries, keys_used, values_used, window_key_value, segment, inside, cache_valid_length, HD
    )
    kept_count = adapter_down_map.shape[0]
    every_adapter = kept_count * row_count
    capacity = max(2, 2 * own_count // every_adapter)
    first_row = column * own_count
    own_rows = lax.dynamic_slice_in_dim(normalized_input, first_row, own_count, 0)
    own_ids = lax.dynamic_slice_in_dim(token_adapter_index[:, 0], first_row, own_count, 0)
    member = (own_ids[:, None] == jnp.arange(every_adapter, dtype=jnp.int32)[None, :]).astype(
        jnp.int32
    )
    before = jnp.cumsum(member, axis=0) - member
    slot_rank = jnp.sum(before * member, axis=1)
    target = own_ids * capacity + slot_rank
    placer = (
        target[None, :] == jnp.arange(every_adapter * capacity, dtype=jnp.int32)[:, None]
    ).astype(jnp.bfloat16)
    outgoing = jnp.dot(placer, own_rows, preferred_element_type=jnp.float32).astype(jnp.bfloat16)
    outgoing = outgoing.reshape(row_count, kept_count, capacity, normalized_input.shape[1])
    reduced_rank_input = jnp.einsum(
        "sakd,adr->sakr",
        lax.all_to_all(outgoing, "row", split_axis=0, concat_axis=0, tiled=True),
        adapter_down_map,
        preferred_element_type=jnp.float32,
    ).astype(jnp.bfloat16)
    answered = jnp.einsum(
        "zjbf,jfm->zjbm", reduced_rank_input, adapter_up_map, preferred_element_type=jnp.float32
    ).astype(jnp.bfloat16)
    returned = lax.all_to_all(answered, "row", split_axis=0, concat_axis=0, tiled=True).reshape(
        every_adapter * capacity, normalized_input.shape[1]
    )
    delta_rows = jnp.dot(jnp.transpose(placer), returned, preferred_element_type=jnp.float32)
    out_term = jnp.dot(
        attended,
        lax.all_gather(output_projection, "row", axis=1, tiled=True),
        preferred_element_type=jnp.float32,
    )
    own_term = lax.dynamic_slice_in_dim(out_term, first_row, own_count, 0) + delta_rows
    out_term = lax.dynamic_update_slice_in_dim(out_term, own_term, first_row, 0)
    attn_share = lax.psum_scatter(
        out_term.astype(jnp.bfloat16), "col", scatter_dimension=0, tiled=True
    ).astype(jnp.float32)
    residual = (inputs.astype(jnp.float32) + attn_share).astype(jnp.bfloat16)
    whole_mixed = lax.all_gather(residual, "col", axis=0, tiled=True)
    normed_mlp = rms_scaled(whole_mixed.astype(jnp.float32), feed_forward_gain).astype(jnp.bfloat16)

    def add_rows(piece):
        return jnp.dot(normed_mlp, piece, preferred_element_type=jnp.float32)

    gate = add_rows(lax.all_gather(gate_projection, "row", axis=0, tiled=True))
    up_part = add_rows(lax.all_gather(up_projection, "row", axis=0, tiled=True))
    hidden = (jax.nn.silu(gate) * up_part).astype(jnp.bfloat16)
    down_term = jnp.dot(
        hidden,
        lax.all_gather(down_projection, "row", axis=1, tiled=True),
        preferred_element_type=jnp.float32,
    )
    mlp_added = lax.psum_scatter(
        down_term.astype(jnp.bfloat16), "col", scatter_dimension=0, tiled=True
    ).astype(jnp.float32)
    return (residual.astype(jnp.float32) + mlp_added).astype(jnp.bfloat16)


def solution(mesh):
    placed = (
        P(("row", "col"), None),
        P(),
        P("row", None, "col"),
        P(None, None, "col"),
        P("col", "row"),
        P("row", None, "col", None),
        P("row"),
        P("row", None),
        P("row", None),
        P("row", None, None),
        P("row", None, None),
        P(),
        P("row", "col"),
        P("row", "col"),
        P("col", "row"),
    )
    return jax.shard_map(
        on_device, mesh=mesh, in_specs=placed, out_specs=P(("row", "col"), None), check_vma=False
    )
```

profile of v0, /device:TPU:4, one launch (start us, length us, event | category | flops | bytes accessed | tf_op | source)
XLA Modules:
  0.0 407.6 jit_solution(15843340719404520123)
XLA Ops:
  6.5 0.7 all-gather.7.cloned.1.call-update
  7.3 0.7 all-gather.9.cloned.1.call-update
  8.0 0.7 broadcast_subtract_fusion
  8.7 0.1 broadcast_in_dim.106
  8.7 0.1 sub.65
  8.8 1.7 reshape.283
  10.5 0.8 reduce-window.4
  11.4 0.7 fusion.50
  12.1 0.1 fusion.40
  12.2 0.1 reduce_window_sum.18
  12.3 0.1 convert_reduce_fusion
  12.4 0.7 fusion.51
  13.0 0.1 select_reduce_fusion.1
  13.1 0.2 select_reduce_fusion
  13.3 0.7 multiply_add_fusion
  14.0 0.6 broadcast_compare_fusion.2
  14.6 1.4 fusion.58
  16.0 36.7 %all-gather.7.cloned.1.call-done = bf16[512,1792]{1,0:T(8,128)(2,1)} async-done(((bf16[64,1792]{1,0:T(8,128)(2,1)}), bf16[512,1792]{1,0:T(8,128)(2,1)}) %all-gather.7.cloned.1.call-update) | async-done | bytes 1835024 | tf_op jit(solution)/shard_map/all_gather | solution.py:147
  52.7 2.1 fusion
  54.8 0.5 fusion.2
  55.3 0.3 convolution_convert_fusion.2
  55.6 0.9 reshape.286
  56.5 7.4 %all-to-all-start = ((bf16[32,2,2,1792]{3,2,1,0:T(2,128)(2,1)}), bf16[32,2,2,1792]{3,2,1,0:T(2,128)(2,1)S(1)}, u32[]{:S(2)}, u32[]{:S(2)}) async-start(bf16[32,2,2,1792]{3,2,1,0:T(2,128)(2,1)} %reshape.286), calls=%async_computation | async-start | bytes 917504 | tf_op jit(solution)/shard_map/all_to_all | solution.py:182
  63.9 0.6 fusion.49
  64.5 0.8 fusion.57
  65.3 8.0 %all-to-all-done = bf16[32,2,2,1792]{3,2,1,0:T(2,128)(2,1)S(1)} async-done(((bf16[32,2,2,1792]{3,2,1,0:T(2,128)(2,1)}), bf16[32,2,2,1792]{3,2,1,0:T(2,128)(2,1)S(1)}, u32[]{:S(2)}, u32[]{:S(2)}) %all-to-all-start) | async-done | bytes 458784 | tf_op jit(solution)/shard_map/all_to_all | solution.py:182
  73.4 0.7 fusion.7
  74.1 1.2 copy.50
  75.4 6.1 %all-to-all-start.1 = ((bf16[32,2,2,1792]{3,2,1,0:T(2,128)(2,1)}), bf16[32,2,2,1792]{3,2,1,0:T(2,128)(2,1)}, u32[]{:S(2)}, u32[]{:S(2)}) async-start(bf16[32,2,2,1792]{3,2,1,0:T(2,128)(2,1)} %copy.50), calls=%async_computation.1 | async-start | bytes 917504 | tf_op jit(solution)/shard_map/all_to_all | solution.py:189
  81.5 0.7 copy.57
  82.2 0.7 copy.58
  83.0 24.7 %all_gather.23 = bf16[224,1792]{0,1:T(8,128)(2,1)S(1)} all-gather(bf16[224,56]{0,1:T(8,128)(2,1)S(1)} %copy-done.11), channel_id=1, replica_groups=mesh['row'=32,'col'=8] {'row'}, dimensions={1}, use_global_device_ids=true | all-gather | bytes 827904 | tf_op jit(solution)/shard_map/all_gather | solution.py:195
  107.7 0.8 compare_and_fusion
  108.4 2.0 reshape.287
  110.4 3.2 fusion.10
  113.7 0.1 slice_bitcast_fusion.1
  113.9 0.4 copy-done.13
  114.4 0.8 fusion.31
  115.2 0.6 fusion.8
  115.8 0.3 copy-done.7
  116.2 0.5 fusion.9
  116.7 1.0 fusion.13
  117.7 0.8 convolution_bitcast_fusion.1
  118.5 0.1 copy-done.9
  118.7 0.8 fusion.16
  119.5 0.7 fusion.59
  120.2 0.3 copy-done.3
  120.5 0.3 fusion.6
  120.8 1.4 convert_element_type.107
  122.3 38.7 %reduce-scatter.3.cloned.1.call-done = bf16[64,1792]{1,0:T(8,128)(2,1)} async-done(((bf16[512,1792]{1,0:T(8,128)(2,1)}), bf16[64,1792]{1,0:T(8,128)(2,1)}) %reduce-scatter.3.cloned.1.call-update) | async-done | bytes 229392 | tf_op jit(solution)/shard_map/reduce_scatter | solution.py:200
  161.0 1.7 add_convert_fusion.1
  162.7 0.5 all-gather.13.cloned.1.call-update
  163.3 0.5 all-gather.15.cloned.1.call-update
  163.9 0.7 all-gather.17.cloned.1.call-update
  164.6 0.3 reduce-scatter.5.cloned.1.call-start
  164.9 37.3 %all-gather.11.cloned.1.call-done = bf16[512,1792]{1,0:T(8,128)(2,1)} async-done(((bf16[64,1792]{1,0:T(8,128)(2,1)}), bf16[512,1792]{1,0:T(8,128)(2,1)}) %all-gather.11.cloned.1.call-update) | async-done | bytes 1835024 | tf_op jit(solution)/shard_map/all_gather | solution.py:204
  202.2 1.9 fusion.3
  204.1 47.1 %all-gather.13.cloned.1.call-done = bf16[1792,512]{1,0:T(8,128)(2,1)} async-done(((bf16[56,512]{1,0:T(8,128)(2,1)}), bf16[1792,512]{1,0:T(8,128)(2,1)}) %all-gather.13.cloned.1.call-update) | async-done | bytes 1835024 | tf_op jit(solution)/shard_map/all_gather | solution.py:210
  251.3 3.2 fusion.24
  254.5 47.1 %all-gather.15.cloned.1.call-done = bf16[1792,512]{1,0:T(8,128)(2,1)} async-done(((bf16[56,512]{1,0:T(8,128)(2,1)}), bf16[1792,512]{1,0:T(8,128)(2,1)}) %all-gather.15.cloned.1.call-update) | async-done | bytes 1835024 | tf_op jit(solution)/shard_map/all_gather | solution.py:211
  301.6 50.5 %all-gather.17.cloned.1.call-done = bf16[512,1792]{0,1:T(8,128)(2,1)} async-done(((bf16[512,56]{0,1:T(8,128)(2,1)}), bf16[512,1792]{0,1:T(8,128)(2,1)}) %all-gather.17.cloned.1.call-update) | async-done | bytes 1835024 | tf_op jit(solution)/shard_map/all_gather | solution.py:215
  352.0 5.6 %convolution_convert_fusion = bf16[512,1792]{1,0:T(8,128)(2,1)} fusion(bf16[512,1792]{0,1:T(8,128)(2,1)} %all-gather.17.cloned.1.call-done, bf16[1792,512]{1,0:T(8,128)(2,1)} %all-gather.15.cloned.1.call-done, f32[512,512]{1,0:T(8,128)S(1)} %fusion.24, bf16[512,1792]{1,0:T(8,128)(2,1)S(1)} %copy-done.4, f32[1792]{0:T(1024)S(1)} %copy-done.22, ...), kind=kOutput, calls=%fused_computation.10 | convolution fusion | flops 1885208576 | bytes 8397824 | tf_op jit(solution)/shard_map/dot_general | solution.py:213
  357.6 41.4 %reduce-scatter.5.cloned.1.call-done = bf16[64,1792]{1,0:T(8,128)(2,1)} async-done(((bf16[512,1792]{1,0:T(8,128)(2,1)}), bf16[64,1792]{1,0:T(8,128)(2,1)}) %reduce-scatter.5.cloned.1.call-update) | async-done | bytes 229392 | tf_op jit(solution)/shard_map/reduce_scatter | solution.py:218
  399.1 1.7 add_convert_fusion
  (62 shorter events, 0.5 us)
Async XLA Ops:
  6.5 66.8 %copy-start = (bf16[2,16,1792]{2,1,0:T(8,128)(2,1)S(1)}, bf16[2,16,1792]{2,1,0:T(8,128)(2,1)}, u32[]{:S(2)}) copy-start(bf16[2,16,1792]{2,1,0:T(8,128)(2,1)} %param.25) | copy-start | bytes 344068
  6.5 48.2 %copy-start.12 = (f32[1792]{0:T(1024)S(1)}, f32[1792]{0:T(1024)}, u32[]{:S(2)}) copy-start(f32[1792]{0:T(1024)} %param.16) | copy-start | bytes 21508
  6.5 46.1 %all-gather.7.cloned.1.call-start = ((), (), s32[]{:S(2)}) async-start(), calls=%async_computation.4 | async-start | bytes 2064384 | tf_op jit(solution)/shard_map/all_gather | solution.py:147
  7.3 103.1 %all-gather.9.cloned.1.call-start = ((), (), s32[]{:S(2)}) async-start(), calls=%async_computation.5 | async-start | bytes 2838528 | tf_op jit(solution)/shard_map/all_gather | solution.py:155
  52.7 2.1 copy-start.1
  55.3 18.1 %copy-start.10 = (bf16[2,1792,16]{1,2,0:T(8,128)(2,1)S(1)}, bf16[2,1792,16]{1,2,0:T(8,128)(2,1)}, u32[]{:S(2)}) copy-start(bf16[2,1792,16]{1,2,0:T(8,128)(2,1)} %param.24) | copy-start | bytes 344068
  56.5 16.9 %all-to-all-start = ((bf16[32,2,2,1792]{3,2,1,0:T(2,128)(2,1)}), bf16[32,2,2,1792]{3,2,1,0:T(2,128)(2,1)S(1)}, u32[]{:S(2)}, u32[]{:S(2)}) async-start(bf16[32,2,2,1792]{3,2,1,0:T(2,128)(2,1)} %reshape.286), calls=%async_computation | async-start | bytes 917504 | tf_op jit(solution)/shard_map/all_to_all | solution.py:182
  65.3 16.2 %copy-start.6 = (bf16[8,1,2,64,112]{4,3,2,1,0:T(8,128)(2,1)S(1)}, bf16[8,1,2,64,112]{4,3,2,1,0:T(8,128)(2,1)}, u32[]{:S(2)}) copy-start(bf16[8,1,2,64,112]{4,3,2,1,0:T(8,128)(2,1)} %get-tuple-element.14) | copy-start | bytes 688132
  65.3 16.9 %copy-start.5 = (bf16[8,1,2,64,112]{4,3,2,1,0:T(8,128)(2,1)S(1)}, bf16[8,1,2,64,112]{4,3,2,1,0:T(8,128)(2,1)}, u32[]{:S(2)}) copy-start(bf16[8,1,2,64,112]{4,3,2,1,0:T(8,128)(2,1)} %get-tuple-element.13) | copy-start | bytes 688132
  65.3 17.6 %copy-start.11 = (bf16[224,56]{0,1:T(8,128)(2,1)S(1)}, bf16[224,56]{0,1:T(8,128)(2,1)}, u32[]{:S(2)}) copy-start(bf16[224,56]{0,1:T(8,128)(2,1)} %param.19) | copy-start | bytes 75268
  74.1 33.6 %copy-start.21 = (pred[512]{0:T(512)(128)(4,1)S(1)}, pred[512]{0:T(512)(128)(4,1)}, u32[]{:S(2)}) copy-start(pred[512]{0:T(512)(128)(4,1)} %fusion.49) | copy-start | bytes 1540
  75.4 33.1 %all-to-all-start.1 = ((bf16[32,2,2,1792]{3,2,1,0:T(2,128)(2,1)}), bf16[32,2,2,1792]{3,2,1,0:T(2,128)(2,1)}, u32[]{:S(2)}, u32[]{:S(2)}) async-start(bf16[32,2,2,1792]{3,2,1,0:T(2,128)(2,1)} %copy.50), calls=%async_computation.1 | async-start | bytes 917504 | tf_op jit(solution)/shard_map/all_to_all | solution.py:189
  81.4 79.5 %reduce-scatter.3.cloned.1.call-start = ((), (), s32[]{:S(2)}) async-start(), calls=%async_computation.6 | async-start | bytes 2064384 | tf_op jit(solution)/shard_map/reduce_scatter | solution.py:200
  113.6 0.7 copy-start.13
  113.7 0.7 copy-start.14
  113.7 0.7 copy-start.15
  113.7 0.7 copy-start.16
  113.7 0.7 copy-start.17
  113.7 0.7 copy-start.18
  113.7 0.7 copy-start.19
  113.7 0.7 copy-start.20
  115.2 1.0 copy-start.7
  117.7 1.0 copy-start.9
  119.5 1.0 copy-start.3
  120.7 40.2 %copy-start.8 = (bf16[64,1792]{1,0:T(8,128)(2,1)S(1)}, bf16[64,1792]{1,0:T(8,128)(2,1)}, u32[]{:S(2)}) copy-start(bf16[64,1792]{1,0:T(8,128)(2,1)} %param.15) | copy-start | bytes 688132
  122.2 129.0 %copy-start.22 = (f32[1792]{0:T(1024)S(1)}, f32[1792]{0:T(1024)}, u32[]{:S(2)}) copy-start(f32[1792]{0:T(1024)} %param.26) | copy-start | bytes 21508
  122.2 79.9 %all-gather.11.cloned.1.call-start = ((), (), s32[]{:S(2)}) async-start(), calls=%async_computation.7 | async-start | bytes 2064384 | tf_op jit(solution)/shard_map/all_gather | solution.py:204
  162.7 88.6 %all-gather.13.cloned.1.call-start = ((), (), s32[]{:S(2)}) async-start(), calls=%async_computation.8 | async-start | bytes 1892352 | tf_op jit(solution)/shard_map/all_gather | solution.py:210
  163.3 138.3 %all-gather.15.cloned.1.call-start = ((), (), s32[]{:S(2)}) async-start(), calls=%async_computation.9 | async-start | bytes 1892352 | tf_op jit(solution)/shard_map/all_gather | solution.py:211
  163.8 188.2 %all-gather.17.cloned.1.call-start = ((), (), s32[]{:S(2)}) async-start(), calls=%async_computation.10 | async-start | bytes 1892352 | tf_op jit(solution)/shard_map/all_gather | solution.py:215
  164.6 234.5 %reduce-scatter.5.cloned.1.call-start = ((), (), s32[]{:S(2)}) async-start(), calls=%async_computation.11 | async-start | bytes 2064384 | tf_op jit(solution)/shard_map/reduce_scatter | solution.py:218
  204.1 147.9 %copy-start.4 = (bf16[512,1792]{1,0:T(8,128)(2,1)S(1)}, bf16[512,1792]{1,0:T(8,128)(2,1)}, u32[]{:S(2)}) copy-start(bf16[512,1792]{1,0:T(8,128)(2,1)} %all-gather.11.cloned.1.call-done) | copy-start | bytes 5505028
  254.5 144.6 %copy-start.2 = (bf16[64,1792]{1,0:T(8,128)(2,1)S(1)}, bf16[64,1792]{1,0:T(8,128)(2,1)}, u32[]{:S(2)}) copy-start(bf16[64,1792]{1,0:T(8,128)(2,1)} %add_convert_fusion.1) | copy-start | bytes 688132
Sparse Core Ops, SparseCore 0:
  9.1 43.4 all-gather.6
  55.3 48.0 all-gather.8
  122.4 38.5 reduce-scatter.2
  162.8 39.3 all-gather.10
  204.6 46.6 all-gather.12
  253.6 47.8 all-gather.14
  304.1 47.8 all-gather.16
  357.8 41.2 reduce-scatter.4
where the time goes:
time: 408 us
  waiting for transfers between devices  310 us (76%)
  blocking collectives  24.7 us (6%)
  matrix products  16.7 us (4%)
  other arithmetic  16.4 us (4%)
  starting transfers between devices  14 us (3%)
  between operations  13.8 us (3%)
  local copies, waits for them, and re-layouts  11.9 us (3%)
    all_gather x1, waiting for transfers between devices, on_device(): lax.all_gather(down_projection, 'row', axis=1, tiled=True)  50.5 us
    all_gather x1, waiting for transfers between devices, on_device(): gate = add_rows(lax.all_gather(gate_projection, 'row', axis=0, tiled=True))  47.1 us
    all_gather x1, waiting for transfers between devices, on_device(): up_part = add_rows(lax.all_gather(up_projection, 'row', axis=0, tiled=True))  47.1 us
    reduce_scatter x1, waiting for transfers between devices, on_device(): lax.psum_scatter(down_term.astype(jnp.bfloat16), 'col', scatter_dimension...  41.4 us
    reduce_scatter x1, waiting for transfers between devices, on_device(): lax.psum_scatter(out_term.astype(jnp.bfloat16), 'col', scatter_dimension=...  38.7 us
    all_gather x1, waiting for transfers between devices, on_device(): whole_mixed = lax.all_gather(residual, 'col', axis=0, tiled=True)  37.3 us
    all_gather x1, waiting for transfers between devices, on_device(): gathered = lax.all_gather(inputs, 'col', axis=0, tiled=True)  36.7 us
    all_gather x1, blocking collectives, on_device(): lax.all_gather(output_projection, 'row', axis=1, tiled=True)  24.7 us
  transfers between devices with their start and end apart: 10, of which 8 were waited for; matrix products, arithmetic and copies ran while one was open for 6% of the time, Pallas kernels for 0%

commit v1 on v0

--- a/solution.py
+++ b/solution.py
@@ -201,7 +201,12 @@
         out_term.astype(jnp.bfloat16), "col", scatter_dimension=0, tiled=True
     ).astype(jnp.float32)
     residual = (inputs.astype(jnp.float32) + attn_share).astype(jnp.bfloat16)
-    whole_mixed = lax.all_gather(residual, "col", axis=0, tiled=True)
+    ring = [residual]
+    for hop in range(7):
+        ring.append(lax.ppermute(ring[-1], "col", [(dev, (dev + 1) % 8) for dev in range(8)]))
+    whole_mixed = jnp.roll(
+        jnp.concatenate(ring[::-1], axis=0), (lax.axis_index("col") + 1) * ring[0].shape[0], axis=0
+    )
     normed_mlp = rms_scaled(whole_mixed.astype(jnp.float32), feed_forward_gain).astype(jnp.bfloat16)
 
     def add_rows(piece):

time: 408 us -> 368 us (0.902)
  waiting for transfers between devices: 310 us -> 268 us
    ppermute x0 -> x7, waiting for transfers between devices: none -> 54.2 us  [on_device(): lax.ppermute(ring[-1], 'col', [(dev, (dev + 1) % 8) for dev in range(8)])]
    all_gather x1, waiting for transfers between devices: 47.1 us -> 0.02 us  [on_device(): gate = add_rows(lax.all_gather(gate_projection, 'row', axis=0, tiled=True))]
    all_gather x1 -> x0, waiting for transfers between devices: 37.3 us -> none  [on_device(): whole_mixed = lax.all_gather(residual, 'col', axis=0, tiled=True)]
    all_gather x1, waiting for transfers between devices: 47.1 us -> 37 us  [on_device(): up_part = add_rows(lax.all_gather(up_projection, 'row', axis=0, tiled=True))]
  transfers between devices with their start and end apart: 10 -> 16, of which waited for: 8 -> 13; matrix products, arithmetic and copies ran while one was open for 6% -> 7% of each run, Pallas kernels for 0% -> 0%
where the time goes in v1:
time: 368 us; the launch traced here: 367 us
  waiting for transfers between devices  268 us (73%)
  blocking collectives  24.8 us (7%)
  matrix products  17.2 us (5%)
  starting transfers between devices  14.9 us (4%)
  other arithmetic  14.3 us (4%)
  between operations  14 us (4%)
  local copies, waits for them, and re-layouts  13.9 us (4%)
    ppermute x7, waiting for transfers between devices, on_device(): lax.ppermute(ring[-1], 'col', [(dev, (dev + 1) % 8) for dev in range(8)])  54.2 us
    all_gather x1, waiting for transfers between devices, on_device(): lax.all_gather(down_projection, 'row', axis=1, tiled=True)  50.3 us
    reduce_scatter x1, waiting for transfers between devices, on_device(): lax.psum_scatter(down_term.astype(jnp.bfloat16), 'col', scatter_dimension...  41.2 us
    reduce_scatter x1, waiting for transfers between devices, on_device(): lax.psum_scatter(out_term.astype(jnp.bfloat16), 'col', scatter_dimension=...  37.6 us
    all_gather x1, waiting for transfers between devices, on_device(): up_part = add_rows(lax.all_gather(up_projection, 'row', axis=0, tiled=True))  37 us
    all_gather x1, waiting for transfers between devices, on_device(): gathered = lax.all_gather(inputs, 'col', axis=0, tiled=True)  36.7 us
    all_gather x1, blocking collectives, on_device(): lax.all_gather(output_projection, 'row', axis=1, tiled=True)  24.8 us
    all_to_all x1, waiting for transfers between devices, on_device(): lax.all_to_all(outgoing, 'row', split_axis=0, concat_axis=0, tiled=True)  8.03 us
  transfers between devices with their start and end apart: 16, of which 13 were waited for; matrix products, arithmetic and copies ran while one was open for 7% of the time, Pallas kernels for 0%

profile of v1, /device:TPU:4, one launch (start us, length us, event | category | flops | bytes accessed | tf_op | source)
XLA Modules:
  0.0 366.7 jit_solution(7715184950158285746)
XLA Ops:
  6.5 0.7 all-gather.6.cloned.1.call-update
  7.3 0.7 all-gather.8.cloned.1.call-update
  8.0 0.7 broadcast_subtract_fusion
  8.8 1.7 reshape.283
  10.5 0.8 reduce-window.4
  11.4 0.7 fusion.54
  12.2 0.1 reduce_window_sum.18
  12.4 0.7 fusion.55
  13.1 0.2 select_reduce_fusion
  13.3 0.7 multiply_add_fusion
  14.0 0.6 broadcast_compare_fusion.2
  14.6 1.4 fusion.62
  16.0 36.7 %all-gather.6.cloned.1.call-done = bf16[512,1792]{1,0:T(8,128)(2,1)} async-done(((bf16[64,1792]{1,0:T(8,128)(2,1)}), bf16[512,1792]{1,0:T(8,128)(2,1)}) %all-gather.6.cloned.1.call-update) | async-done | bytes 1835024 | tf_op jit(solution)/shard_map/all_gather | solution.py:147
  52.7 2.1 fusion
  54.8 0.5 fusion.2
  55.3 0.3 convolution_convert_fusion.2
  55.6 0.9 reshape.286
  56.5 7.4 %all-to-all-start = ((bf16[32,2,2,1792]{3,2,1,0:T(2,128)(2,1)}), bf16[32,2,2,1792]{3,2,1,0:T(2,128)(2,1)S(1)}, u32[]{:S(2)}, u32[]{:S(2)}) async-start(bf16[32,2,2,1792]{3,2,1,0:T(2,128)(2,1)} %reshape.286), calls=%async_computation | async-start | bytes 917504 | tf_op jit(solution)/shard_map/all_to_all | solution.py:182
  63.9 0.6 fusion.53
  64.5 0.8 fusion.61
  65.3 8.0 %all-to-all-done = bf16[32,2,2,1792]{3,2,1,0:T(2,128)(2,1)S(1)} async-done(((bf16[32,2,2,1792]{3,2,1,0:T(2,128)(2,1)}), bf16[32,2,2,1792]{3,2,1,0:T(2,128)(2,1)S(1)}, u32[]{:S(2)}, u32[]{:S(2)}) %all-to-all-start) | async-done | bytes 458784 | tf_op jit(solution)/shard_map/all_to_all | solution.py:182
  73.4 0.7 fusion.7
  74.1 1.2 copy.50
  75.4 6.1 %all-to-all-start.1 = ((bf16[32,2,2,1792]{3,2,1,0:T(2,128)(2,1)}), bf16[32,2,2,1792]{3,2,1,0:T(2,128)(2,1)}, u32[]{:S(2)}, u32[]{:S(2)}) async-start(bf16[32,2,2,1792]{3,2,1,0:T(2,128)(2,1)} %copy.50), calls=%async_computation.1 | async-start | bytes 917504 | tf_op jit(solution)/shard_map/all_to_all | solution.py:189
  81.5 0.7 copy.57
  82.2 0.7 copy.58
  82.9 24.8 %all_gather.20 = bf16[224,1792]{0,1:T(8,128)(2,1)S(1)} all-gather(bf16[224,56]{0,1:T(8,128)(2,1)S(1)} %copy-done.10), channel_id=1, replica_groups=mesh['row'=32,'col'=8] {'row'}, dimensions={1}, use_global_device_ids=true | all-gather | bytes 827904 | tf_op jit(solution)/shard_map/all_gather | solution.py:195
  107.7 0.8 compare_and_fusion
  108.5 2.0 reshape.287
  110.4 3.2 fusion.10
  113.9 0.4 copy-done.12
  114.4 0.8 fusion.28
  115.2 0.6 fusion.8
  115.9 0.3 copy-done.6
  116.2 0.5 fusion.9
  116.7 1.0 fusion.13
  117.8 0.8 convolution_bitcast_fusion.1
  118.5 0.1 copy-done.8
  118.7 0.8 fusion.15
  119.5 0.7 fusion.63
  120.2 0.3 copy-done.2
  120.5 0.3 fusion.6
  120.8 1.4 convert_element_type.107
  122.3 0.5 all-gather.10.cloned.1.call-update
  122.9 0.5 all-gather.12.cloned.1.call-update
  123.5 37.6 %reduce-scatter.3.cloned.1.call-done = bf16[64,1792]{1,0:T(8,128)(2,1)} async-done(((bf16[512,1792]{1,0:T(8,128)(2,1)}), bf16[64,1792]{1,0:T(8,128)(2,1)}) %reduce-scatter.3.cloned.1.call-update) | async-done | bytes 229392 | tf_op jit(solution)/shard_map/reduce_scatter | solution.py:200
  161.1 1.0 add_convert_fusion.1
  162.1 1.1 collective-permute-start
  163.1 8.2 %collective-permute-done = bf16[64,1792]{1,0:T(8,128)(2,1)S(1)} collective-permute-done((bf16[64,1792]{1,0:T(8,128)(2,1)S(1)}, bf16[64,1792]{1,0:T(8,128)(2,1)S(1)}, u32[]{:S(2)}, u32[]{:S(2)}) %collective-permute-start) | collective-permute-done | bytes 229408 | tf_op jit(solution)/shard_map/ppermute | solution.py:206
  171.3 0.1 collective-permute-start.1
  171.4 8.9 %collective-permute-done.1 = bf16[64,1792]{1,0:T(8,128)(2,1)S(1)} collective-permute-done((bf16[64,1792]{1,0:T(8,128)(2,1)S(1)}, bf16[64,1792]{1,0:T(8,128)(2,1)S(1)}, u32[]{:S(2)}, u32[]{:S(2)}) %collective-permute-start.1) | collective-permute-done | bytes 229408 | tf_op jit(solution)/shard_map/ppermute | solution.py:206
  180.4 8.2 %collective-permute-done.2 = bf16[64,1792]{1,0:T(8,128)(2,1)S(1)} collective-permute-done((bf16[64,1792]{1,0:T(8,128)(2,1)S(1)}, bf16[64,1792]{1,0:T(8,128)(2,1)S(1)}, u32[]{:S(2)}, u32[]{:S(2)}) %collective-permute-start.2) | collective-permute-done | bytes 229408 | tf_op jit(solution)/shard_map/ppermute | solution.py:206
  188.6 7.3 %collective-permute-done.3 = bf16[64,1792]{1,0:T(8,128)(2,1)S(1)} collective-permute-done((bf16[64,1792]{1,0:T(8,128)(2,1)S(1)}, bf16[64,1792]{1,0:T(8,128)(2,1)S(1)}, u32[]{:S(2)}, u32[]{:S(2)}) %collective-permute-start.3) | collective-permute-done | bytes 229408 | tf_op jit(solution)/shard_map/ppermute | solution.py:206
  195.9 7.2 %collective-permute-done.4 = bf16[64,1792]{1,0:T(8,128)(2,1)S(1)} collective-permute-done((bf16[64,1792]{1,0:T(8,128)(2,1)S(1)}, bf16[64,1792]{1,0:T(8,128)(2,1)S(1)}, u32[]{:S(2)}, u32[]{:S(2)}) %collective-permute-start.4) | collective-permute-done | bytes 229408 | tf_op jit(solution)/shard_map/ppermute | solution.py:206
  203.1 7.2 %collective-permute-done.5 = bf16[64,1792]{1,0:T(8,128)(2,1)S(1)} collective-permute-done((bf16[64,1792]{1,0:T(8,128)(2,1)S(1)}, bf16[64,1792]{1,0:T(8,128)(2,1)S(1)}, u32[]{:S(2)}, u32[]{:S(2)}) %collective-permute-start.5) | collective-permute-done | bytes 229408 | tf_op jit(solution)/shard_map/ppermute | solution.py:206
  210.4 7.1 %collective-permute-done.6 = bf16[64,1792]{1,0:T(8,128)(2,1)S(1)} collective-permute-done((bf16[64,1792]{1,0:T(8,128)(2,1)S(1)}, bf16[64,1792]{1,0:T(8,128)(2,1)S(1)}, u32[]{:S(2)}, u32[]{:S(2)}) %collective-permute-start.6) | collective-permute-done | bytes 229408 | tf_op jit(solution)/shard_map/ppermute | solution.py:206
  218.0 1.8 copy-done.3
  219.8 0.4 fusion.3
  220.2 3.2 fusion.33
  223.5 37.0 %all-gather.12.cloned.1.call-done = bf16[1792,512]{1,0:T(8,128)(2,1)} async-done(((bf16[56,512]{1,0:T(8,128)(2,1)}), bf16[1792,512]{1,0:T(8,128)(2,1)}) %all-gather.12.cloned.1.call-update) | async-done | bytes 1835024 | tf_op jit(solution)/shard_map/all_gather | solution.py:216
  260.5 50.3 %all-gather.14.cloned.1.call-done = bf16[512,1792]{0,1:T(8,128)(2,1)} async-done(((bf16[512,56]{0,1:T(8,128)(2,1)}), bf16[512,1792]{0,1:T(8,128)(2,1)}) %all-gather.14.cloned.1.call-update) | async-done | bytes 1835024 | tf_op jit(solution)/shard_map/all_gather | solution.py:220
  310.8 6.1 %convolution_convert_fusion = bf16[512,1792]{1,0:T(8,128)(2,1)} fusion(bf16[512,1792]{0,1:T(8,128)(2,1)} %all-gather.14.cloned.1.call-done, f32[512,512]{1,0:T(8,128)S(1)} %fusion.33, bf16[1792,512]{1,0:T(8,128)(2,1)} %all-gather.12.cloned.1.call-done, f32[1792]{0:T(1024)S(1)} %copy-done.21, f32[512]{0:T(512)S(1)} %add_rsqrt_fusion, ...), kind=kOutput, calls=%fused_computation.10 | convolution fusion | flops 1885208576 | bytes 8397828 | tf_op jit(solution)/shard_map/dot_general | solution.py:218
  316.9 41.2 %reduce-scatter.5.cloned.1.call-done = bf16[64,1792]{1,0:T(8,128)(2,1)} async-done(((bf16[512,1792]{1,0:T(8,128)(2,1)}), bf16[64,1792]{1,0:T(8,128)(2,1)}) %reduce-scatter.5.cloned.1.call-update) | async-done | bytes 229392 | tf_op jit(solution)/shard_map/reduce_scatter | solution.py:223
  358.1 1.7 add_convert_fusion
  (87 shorter events, 1.3 us)
Async XLA Ops:
  6.5 66.8 %copy-start = (bf16[2,16,1792]{2,1,0:T(8,128)(2,1)S(1)}, bf16[2,16,1792]{2,1,0:T(8,128)(2,1)}, u32[]{:S(2)}) copy-start(bf16[2,16,1792]{2,1,0:T(8,128)(2,1)} %param.25) | copy-start | bytes 344068
  6.5 48.2 %copy-start.11 = (f32[1792]{0:T(1024)S(1)}, f32[1792]{0:T(1024)}, u32[]{:S(2)}) copy-start(f32[1792]{0:T(1024)} %param.16) | copy-start | bytes 21508
  6.5 46.1 %all-gather.6.cloned.1.call-start = ((), (), s32[]{:S(2)}) async-start(), calls=%async_computation.4 | async-start | bytes 2064384 | tf_op jit(solution)/shard_map/all_gather | solution.py:147
  7.3 103.2 %all-gather.8.cloned.1.call-start = ((), (), s32[]{:S(2)}) async-start(), calls=%async_computation.5 | async-start | bytes 2838528 | tf_op jit(solution)/shard_map/all_gather | solution.py:155
  52.7 2.1 copy-start.1
  55.3 18.1 %copy-start.9 = (bf16[2,1792,16]{1,2,0:T(8,128)(2,1)S(1)}, bf16[2,1792,16]{1,2,0:T(8,128)(2,1)}, u32[]{:S(2)}) copy-start(bf16[2,1792,16]{1,2,0:T(8,128)(2,1)} %param.24) | copy-start | bytes 344068
  56.5 16.9 %all-to-all-start = ((bf16[32,2,2,1792]{3,2,1,0:T(2,128)(2,1)}), bf16[32,2,2,1792]{3,2,1,0:T(2,128)(2,1)S(1)}, u32[]{:S(2)}, u32[]{:S(2)}) async-start(bf16[32,2,2,1792]{3,2,1,0:T(2,128)(2,1)} %reshape.286), calls=%async_computation | async-start | bytes 917504 | tf_op jit(solution)/shard_map/all_to_all | solution.py:182
  65.3 16.2 %copy-start.5 = (bf16[8,1,2,64,112]{4,3,2,1,0:T(8,128)(2,1)S(1)}, bf16[8,1,2,64,112]{4,3,2,1,0:T(8,128)(2,1)}, u32[]{:S(2)}) copy-start(bf16[8,1,2,64,112]{4,3,2,1,0:T(8,128)(2,1)} %get-tuple-element.14) | copy-start | bytes 688132
  65.3 16.9 %copy-start.4 = (bf16[8,1,2,64,112]{4,3,2,1,0:T(8,128)(2,1)S(1)}, bf16[8,1,2,64,112]{4,3,2,1,0:T(8,128)(2,1)}, u32[]{:S(2)}) copy-start(bf16[8,1,2,64,112]{4,3,2,1,0:T(8,128)(2,1)} %get-tuple-element.13) | copy-start | bytes 688132
  65.3 17.6 %copy-start.10 = (bf16[224,56]{0,1:T(8,128)(2,1)S(1)}, bf16[224,56]{0,1:T(8,128)(2,1)}, u32[]{:S(2)}) copy-start(bf16[224,56]{0,1:T(8,128)(2,1)} %param.19) | copy-start | bytes 75268
  74.1 33.6 %copy-start.20 = (pred[512]{0:T(512)(128)(4,1)S(1)}, pred[512]{0:T(512)(128)(4,1)}, u32[]{:S(2)}) copy-start(pred[512]{0:T(512)(128)(4,1)} %fusion.53) | copy-start | bytes 1540
  75.4 33.1 %all-to-all-start.1 = ((bf16[32,2,2,1792]{3,2,1,0:T(2,128)(2,1)}), bf16[32,2,2,1792]{3,2,1,0:T(2,128)(2,1)}, u32[]{:S(2)}, u32[]{:S(2)}) async-start(bf16[32,2,2,1792]{3,2,1,0:T(2,128)(2,1)} %copy.50), calls=%async_computation.1 | async-start | bytes 917504 | tf_op jit(solution)/shard_map/all_to_all | solution.py:189
  81.4 79.6 %reduce-scatter.3.cloned.1.call-start = ((), (), s32[]{:S(2)}) async-start(), calls=%async_computation.6 | async-start | bytes 2064384 | tf_op jit(solution)/shard_map/reduce_scatter | solution.py:200
  113.7 0.7 copy-start.12
  113.7 0.7 copy-start.13
  113.7 0.7 copy-start.14
  113.7 0.7 copy-start.15
  113.7 0.7 copy-start.16
  113.7 0.7 copy-start.17
  113.7 0.7 copy-start.18
  113.7 0.7 copy-start.19
  115.2 1.0 copy-start.6
  117.7 1.0 copy-start.8
  119.5 1.0 copy-start.2
  122.2 38.8 %copy-start.7 = (bf16[64,1792]{1,0:T(8,128)(2,1)S(1)}, bf16[64,1792]{1,0:T(8,128)(2,1)}, u32[]{:S(2)}) copy-start(bf16[64,1792]{1,0:T(8,128)(2,1)} %param.15) | copy-start | bytes 688132
  122.2 98.0 %all-gather.10.cloned.1.call-start = ((), (), s32[]{:S(2)}) async-start(), calls=%async_computation.7 | async-start | bytes 1892352 | tf_op jit(solution)/shard_map/all_gather | solution.py:215
  122.8 137.7 %all-gather.12.cloned.1.call-start = ((), (), s32[]{:S(2)}) async-start(), calls=%async_computation.8 | async-start | bytes 1892352 | tf_op jit(solution)/shard_map/all_gather | solution.py:216
  123.4 187.4 %all-gather.14.cloned.1.call-start = ((), (), s32[]{:S(2)}) async-start(), calls=%async_computation.9 | async-start | bytes 1892352 | tf_op jit(solution)/shard_map/all_gather | solution.py:220
  162.1 9.3 %collective-permute-start = (bf16[64,1792]{1,0:T(8,128)(2,1)S(1)}, bf16[64,1792]{1,0:T(8,128)(2,1)S(1)}, u32[]{:S(2)}, u32[]{:S(2)}) collective-permute-start(bf16[64,1792]{1,0:T(8,128)(2,1)S(1)} %add_convert_fusion.1), channel_id=1, source_target_pairs={{0,1},{1,2},{2,3},{3,4},{4,5},{5,6},{6,7},{7,0},{8,9},{9,10},{10,1... | collective-permute-start | bytes 688136 | tf_op jit(solution)/shard_map/ppermute | solution.py:206
  171.3 9.0 %collective-permute-start.1 = (bf16[64,1792]{1,0:T(8,128)(2,1)S(1)}, bf16[64,1792]{1,0:T(8,128)(2,1)S(1)}, u32[]{:S(2)}, u32[]{:S(2)}) collective-permute-start(bf16[64,1792]{1,0:T(8,128)(2,1)S(1)} %collective-permute-done), channel_id=1, source_target_pairs={{0,1},{1,2},{2,3},{3,4},{4,5},{5,6},{6,7},{7,0},{8,9},{9,10},{10,1... | collective-permute-start | bytes 688136 | tf_op jit(solution)/shard_map/ppermute | solution.py:206
  180.4 8.2 %collective-permute-start.2 = (bf16[64,1792]{1,0:T(8,128)(2,1)S(1)}, bf16[64,1792]{1,0:T(8,128)(2,1)S(1)}, u32[]{:S(2)}, u32[]{:S(2)}) collective-permute-start(bf16[64,1792]{1,0:T(8,128)(2,1)S(1)} %collective-permute-done.1), channel_id=1, source_target_pairs={{0,1},{1,2},{2,3},{3,4},{4,5},{5,6},{6,7},{7,0},{8,9},{9,10},{10,1... | collective-permute-start | bytes 688136 | tf_op jit(solution)/shard_map/ppermute | solution.py:206
  188.6 7.3 %collective-permute-start.3 = (bf16[64,1792]{1,0:T(8,128)(2,1)S(1)}, bf16[64,1792]{1,0:T(8,128)(2,1)S(1)}, u32[]{:S(2)}, u32[]{:S(2)}) collective-permute-start(bf16[64,1792]{1,0:T(8,128)(2,1)S(1)} %collective-permute-done.2), channel_id=1, source_target_pairs={{0,1},{1,2},{2,3},{3,4},{4,5},{5,6},{6,7},{7,0},{8,9},{9,10},{10,1... | collective-permute-start | bytes 688136 | tf_op jit(solution)/shard_map/ppermute | solution.py:206
  195.9 7.2 %collective-permute-start.4 = (bf16[64,1792]{1,0:T(8,128)(2,1)S(1)}, bf16[64,1792]{1,0:T(8,128)(2,1)S(1)}, u32[]{:S(2)}, u32[]{:S(2)}) collective-permute-start(bf16[64,1792]{1,0:T(8,128)(2,1)S(1)} %collective-permute-done.3), channel_id=1, source_target_pairs={{0,1},{1,2},{2,3},{3,4},{4,5},{5,6},{6,7},{7,0},{8,9},{9,10},{10,1... | collective-permute-start | bytes 688136 | tf_op jit(solution)/shard_map/ppermute | solution.py:206
  203.1 7.2 %collective-permute-start.5 = (bf16[64,1792]{1,0:T(8,128)(2,1)S(1)}, bf16[64,1792]{1,0:T(8,128)(2,1)S(1)}, u32[]{:S(2)}, u32[]{:S(2)}) collective-permute-start(bf16[64,1792]{1,0:T(8,128)(2,1)S(1)} %collective-permute-done.4), channel_id=1, source_target_pairs={{0,1},{1,2},{2,3},{3,4},{4,5},{5,6},{6,7},{7,0},{8,9},{9,10},{10,1... | collective-permute-start | bytes 688136 | tf_op jit(solution)/shard_map/ppermute | solution.py:206
  210.3 7.2 %collective-permute-start.6 = (bf16[64,1792]{1,0:T(8,128)(2,1)S(1)}, bf16[64,1792]{1,0:T(8,128)(2,1)S(1)}, u32[]{:S(2)}, u32[]{:S(2)}) collective-permute-start(bf16[64,1792]{1,0:T(8,128)(2,1)S(1)} %collective-permute-done.5), channel_id=1, source_target_pairs={{0,1},{1,2},{2,3},{3,4},{4,5},{5,6},{6,7},{7,0},{8,9},{9,10},{10,1... | collective-permute-start | bytes 688136 | tf_op jit(solution)/shard_map/ppermute | solution.py:206
  210.4 147.8 %reduce-scatter.5.cloned.1.call-start = ((), (), s32[]{:S(2)}) async-start(), calls=%async_computation.10 | async-start | bytes 2064384 | tf_op jit(solution)/shard_map/reduce_scatter | solution.py:223
  217.8 2.4 copy-start.21
  218.0 1.8 copy-start.3
Sparse Core Ops, SparseCore 0:
  9.1 43.4 all-gather.5
  55.3 48.0 all-gather.7
  122.4 38.6 reduce-scatter.2
  163.5 46.7 all-gather.9
  212.6 47.8 all-gather.11
  262.9 47.8 all-gather.13
  317.1 41.0 reduce-scatter.4
